TPU v7x, 256 devices: a whole 4x4x8 slice. The times are simulated.
256 devices in a mesh: tm: 32 (over y_hi, z, core), head: 4 (over x), rep: 2 (over y_lo).
Axes of the slice: x: 4, y: 4 (y_hi: 2, y_lo: 2; y = y_hi * 2 + y_lo), z: 8, core: 2. Of those that a mesh axis runs over, the one named last changes fastest.
Arguments:
- queries: bfloat16 [32768, 1536], P(('tm', 'rep'), 'head'), may hold values from -8 to 8
- kv_cache: bfloat16 [32768, 2, 1536], P('tm', None, 'head'), may hold values from -8 to 8
- out_weight: bfloat16 [1536, 3072], P('head'), may hold values from -0.15625 to 0.15625
- fetch_list: int32 [64, 32], P(('tm', 'rep')), may hold values from 0 to 247, as said below
- tile_lists: int32 [256, 16], P(('tm', 'rep')), may hold values from 0 to 31, as said below
- event_offsets: int32 [256], P(('tm', 'rep')), may hold values from 0 to 7
Outputs:
- mixed: bfloat16 [32768, 3072], P(('tm', 'rep'), 'head')
Inputs may be any that keep to these rules, and one draw needn't show every extreme that they name: `fetch_list`: each row names 32 distinct blocks, all with ids below (31) * 8, so none of the newest ones; one row names at most 2 blocks of one owner, and every row names exactly 2 blocks of some owner. `tile_lists`: each row names 16 distinct positions; the tiles of one device together name every position of its row of fetch_list.
All inputs are finite; a program needn't handle non-finite values.
Results may differ from a plain program's by a relative error of at most 0.013.
Values may be sent and summed in bfloat16 or wider, within the bound.
No kernel may reach another device: no remote copies, remote signals or barrier semaphores. Data moves between devices by JAX's collectives and lax.ppermute only.
A program may use at most 128 MiB of HBM per device.

v0:
```python
import math
import jax
import jax.numpy as jnp
from jax import lax
from jax.sharding import PartitionSpec as P

DH = 128
TILE = 128
CB_DEV = 8
CAP = 2


def from_root(shard, axis, root):
    mine = lax.axis_index(axis) == root
    return lax.psum(jnp.where(mine, shard, jnp.zeros_like(shard)), axis)


def owner_ranks(owners):
    entry_count = owners.shape[-1]
    index_row = jnp.arange(entry_count, dtype=jnp.int32)
    same_owner = owners[..., None, :] == owners[..., :, None]
    earlier = index_row[None, :] < index_row[:, None]
    return jnp.sum(same_owner & earlier, axis=-1)


def outgoing(requests, wanted, block_rows, me_owner):
    owners = requests // CB_DEV
    slot_ids = requests % CB_DEV
    rank_ids = owner_ranks(owners)
    is_mine = owners == me_owner
    hit_table = is_mine[:, :, None] & (rank_ids[:, :, None] == wanted[None, None, :])
    chosen = jnp.sum(jnp.where(hit_table, slot_ids[:, :, None], 0), axis=1)
    in_use = jnp.any(hit_table, axis=1)
    picked = jnp.take(block_rows, chosen, axis=0)
    return jnp.where(in_use[:, :, None, None, None], picked, jnp.zeros_like(picked))


def shards(queries, kv_cache, out_weight, fetch_list, tile_lists, event_offsets):
    me_owner = lax.axis_index("tm")
    feature_width = kv_cache.shape[2]
    head_count = feature_width // DH
    block_rows = kv_cache.reshape(CB_DEV, -1, 2, feature_width)
    block_len = block_rows.shape[1]
    own_owners = fetch_list[0] // CB_DEV
    own_ranks = owner_ranks(own_owners)
    requests = lax.all_gather(fetch_list, "tm", axis=0, tiled=True)
    outbound = outgoing(requests, jnp.arange(CAP, dtype=jnp.int32), block_rows, me_owner)
    arrived = lax.all_to_all(outbound, "tm", split_axis=0, concat_axis=0, tiled=True)
    flat_blocks = arrived.reshape(-1, block_len, 2, feature_width)
    fetched = jnp.take(flat_blocks, own_owners * CAP + own_ranks, axis=0)
    newest = lax.axis_size("tm") - 1
    panel_rows = from_root(kv_cache, "tm", newest)
    panel_keys = panel_rows[:, 0].reshape(-1, head_count, DH)
    panel_values = panel_rows[:, 1].reshape(-1, head_count, DH)
    slab_rows = panel_keys.shape[0]
    tile_count = queries.shape[0] // TILE
    per_step = math.gcd(tile_count, 4)
    query_groups = queries.reshape(tile_count // per_step, per_step, TILE, head_count, DH)
    list_groups = tile_lists.reshape(tile_count // per_step, per_step, -1)
    offset_groups = event_offsets.reshape(tile_count // per_step, per_step)
    score_scale = 1.0 / math.sqrt(DH)
    positions = jnp.arange(slab_rows, dtype=jnp.int32)

    def attend(pieces):
        query_block, list_rows, offsets = pieces
        picked = jnp.take(fetched, list_rows, axis=0).reshape(per_step, -1, 2, feature_width)
        far_keys = picked[:, :, 0].reshape(per_step, -1, head_count, DH)
        far_values = picked[:, :, 1].reshape(per_step, -1, head_count, DH)
        far_scores = (
            jnp.einsum("gqhd,gkhd->ghqk", query_block, far_keys, preferred_element_type=jnp.float32)
            * score_scale
        )
        near_scores = (
            jnp.einsum(
                "gqhd,khd->ghqk", query_block, panel_keys, preferred_element_type=jnp.float32
            )
            * score_scale
        )
        visible = positions[None, :] < (CB_DEV - offsets)[:, None] * block_len
        near_scores = jnp.where(visible[:, None, None, :], near_scores, -1e30)
        row_max = jnp.maximum(jnp.max(far_scores, axis=-1), jnp.max(near_scores, axis=-1))
        far_weights = jnp.exp(far_scores - row_max[..., None])
        near_weights = jnp.exp(near_scores - row_max[..., None])
        denom_sum = jnp.sum(far_weights, axis=-1) + jnp.sum(near_weights, axis=-1)
        blended = jnp.einsum(
            "ghqk,gkhd->gqhd",
            far_weights.astype(jnp.bfloat16),
            far_values,
            preferred_element_type=jnp.float32,
        )
        blended = blended + jnp.einsum(
            "ghqk,khd->gqhd",
            near_weights.astype(jnp.bfloat16),
            panel_values,
            preferred_element_type=jnp.float32,
        )
        blended = blended / jnp.transpose(denom_sum, (0, 2, 1))[..., None]
        return blended.astype(jnp.bfloat16).reshape(per_step, TILE, head_count * DH)

    attended = lax.map(attend, (query_groups, list_groups, offset_groups)).reshape(
        -1, head_count * DH
    )
    partial_value = jnp.dot(attended, out_weight, preferred_element_type=jnp.float32)
    return lax.psum_scatter(
        partial_value.astype(jnp.bfloat16), "head", scatter_dimension=1, tiled=True
    )


def solution(mesh):
    placed = (
        P(("tm", "rep"), "head"),
        P("tm", None, "head"),
        P("head", None),
        P(("tm", "rep"), None),
        P(("tm", "rep"), None),
        P(("tm", "rep")),
    )
    return jax.shard_map(
        shards, mesh=mesh, in_specs=placed, out_specs=P(("tm", "rep"), "head"), check_vma=False
    )
```

profile of v0, /device:TPU:1, one launch (start us, length us, event | category | flops | bytes accessed | tf_op | source)
XLA Modules:
  0.0 600.0 jit_solution(15882582718426881978)
XLA Ops:
  6.5 46.3 %all-gather = s32[32,1,32]{2,1,0:T(1,128)S(1)} all-gather(s32[1,1,32]{2,1,0:T(1,128)} %bitcast.112), channel_id=1, replica_groups=mesh['tm'=32,'head'=4,'rep'=2] {'tm'}, dimensions={0}, use_global_device_ids=true | all-gather | bytes 4224 | tf_op jit(solution)/shard_map/all_gather | solution.py:46
  54.1 29.4 %gather_fusion = bf16[64,128,2,384]{3,2,1,0:T(2,128)(2,1)} fusion(bf16[8,128,2,384]{3,2,1,0:T(2,128)(2,1)} %bitcast.101, s32[1024]{0:T(1024)S(1)} %pad_clamp_fusion.2), kind=kCustom, calls=%fused_computation | custom fusion | bytes 25166080 | tf_op jit(solution)/shard_map/jit(_take)/gather | solution.py:34
  83.5 11.5 %copy.119 = bf16[64,128,2,384]{3,1,2,0:T(8,128)(2,1)} copy(bf16[64,128,2,384]{3,2,1,0:T(2,128)(2,1)} %gather_fusion) | data formatting | bytes 25165824 | tf_op jit(solution)/shard_map/jit(_take)/gather | solution.py:34
  95.3 11.0 %select_select_fusion = bf16[32,2,128,2,384]{4,2,3,1,0:T(8,128)(2,1)} fusion(bf16[32,2,128,2,384]{4,2,3,1,0:T(8,128)(2,1)} %bitcast.102, pred[32,2]{1,0:T(8,128)(4,1)S(1)} %copy.117, pred[32,2]{1,0:T(8,128)(4,1)S(1)} %copy.116), kind=kLoop, calls=%fused_computation.7 | loop fusion | flops 12582912 | bytes 25165952 | tf_op jit(solution)/shard_map/jit(_where)/select_n | solution.py:35
  106.3 4.8 all-to-all-start
  111.3 5.0 copy.126
  116.3 1.3 broadcast_select_fusion.1
  119.7 346.7 %all-reduce.2.cloned.1.call-done = bf16[1024,2,384]{0,2,1:T(8,128)(2,1)} async-done(((bf16[1024,2,384]{0,2,1:T(8,128)(2,1)}), bf16[1024,2,384]{0,2,1:T(8,128)(2,1)}) %all-reduce.2.cloned.1.call-update) | async-done | bytes 1572880 | tf_op jit(solution)/shard_map/psum | solution.py:15
  466.4 1.5 fusion.42
  467.9 4.3 fusion.9
  472.2 8.7 %gather_fusion.1 = bf16[32,128,2,384]{3,1,2,0:T(8,128)(2,1)} fusion(bf16[64,128,2,384]{3,1,2,0:T(8,128)(2,1)} %bitcast.7, s32[1024]{0:T(1024)} %pad_clamp_fusion.1), kind=kCustom, calls=%fused_computation.1 | custom fusion | bytes 12583040 | tf_op jit(solution)/shard_map/jit(_take)/gather | solution.py:50
  480.9 6.2 %broadcast_select_fusion = bf16[32,128,2,384]{3,1,2,0:T(8,128)(2,1)} fusion(bf16[32,128,2,384]{3,1,2,0:T(8,128)(2,1)} %gather_fusion.1, pred[32]{0:T(512)(128)(4,1)} %compare_and_fusion.1), kind=kLoop, calls=%fused_computation.15 | loop fusion | flops 3145728 | bytes 12582944 | tf_op jit(solution)/shard_map/jit(_take)/select_n | solution.py:50
  487.1 9.9 %gather_fusion.2 = bf16[64,128,2,384]{3,1,2,0:T(8,128)(2,1)} fusion(bf16[32,128,2,384]{3,1,2,0:T(8,128)(2,1)} %broadcast_select_fusion, s32[1024]{0:T(1024)S(1)} %pad_clamp_fusion), kind=kCustom, calls=%fused_computation.2 | custom fusion | bytes 25166080 | tf_op jit(solution)/shard_map/while/body/eval_jaxpr/jit(_take)/gather | solution.py:66
  496.9 7.0 %copy.120 = bf16[64,128,2,384]{3,1,0,2:T(8,128)(2,1)S(1)} copy(bf16[64,128,2,384]{3,1,2,0:T(8,128)(2,1)} %gather_fusion.2) | data formatting | bytes 25165824 | tf_op jit(solution)/shard_map/while/body/eval_jaxpr/jit(_take)/gather | solution.py:66
  504.0 3.0 bitcast_select_fusion
  506.9 5.7 fusion.41
  512.7 8.7 %copy.121 = bf16[4,2048,1,384]{1,3,0,2:T(8,128)(2,1)} copy(bf16[4,2048,1,384]{3,1,0,2:T(8,128)(2,1)} %get-tuple-element.24) | data formatting | bytes 12582912 | tf_op jit(solution)/shard_map/while/body/eval_jaxpr/slice | solution.py:68
  521.3 8.6 %copy.122 = bf16[4,2048,1,384]{1,3,0,2:T(8,128)(2,1)} copy(bf16[4,2048,1,384]{3,1,0,2:T(8,128)(2,1)} %get-tuple-element.23) | data formatting | bytes 12582912 | tf_op jit(solution)/shard_map/while/body/eval_jaxpr/slice | solution.py:67
  529.9 4.7 bitcast_reduce_fusion
  534.6 2.1 fusion.1
  536.7 5.4 fusion.12
  542.1 4.7 fusion.7
  547.9 3.5 convolution_convert_fusion
  551.4 41.8 %reduce-scatter.2.cloned.1.call-done = bf16[512,768]{1,0:T(8,128)(2,1)} async-done(((bf16[512,3072]{1,0:T(8,128)(2,1)}), bf16[512,768]{1,0:T(8,128)(2,1)}) %reduce-scatter.2.cloned.1.call-update) | async-done | bytes 786448 | tf_op jit(solution)/shard_map/reduce_scatter | solution.py:104
  (51 shorter events, 4.6 us)
Async XLA Ops:
  6.5 541.3 %copy-start = (bf16[384,3072]{1,0:T(8,128)(2,1)S(1)}, bf16[384,3072]{1,0:T(8,128)(2,1)}, u32[]{:S(2)}) copy-start(bf16[384,3072]{1,0:T(8,128)(2,1)} %param.8) | copy-start | bytes 7077892
  106.3 365.9 %all-to-all-start = ((bf16[32,2,128,2,384]{4,2,3,1,0:T(8,128)(2,1)}), bf16[32,2,128,2,384]{4,2,3,1,0:T(8,128)(2,1)}, u32[]{:S(2)}, u32[]{:S(2)}) async-start(bf16[32,2,128,2,384]{4,2,3,1,0:T(8,128)(2,1)} %select_select_fusion), calls=%async_computation | async-start | bytes 25165824 | tf_op jit(solution)/shard_map/all_to_all | solution.py:48
  111.2 6.5 %copy-start.3 = (s32[4,16]{1,0:T(4,128)S(1)}, s32[4,16]{1,0:T(4,128)}, u32[]{:S(2)}) copy-start(s32[4,16]{1,0:T(4,128)} %param.10) | copy-start | bytes 772
  111.2 6.7 %copy-start.1 = (bf16[512,384]{1,0:T(8,128)(2,1)S(1)}, bf16[512,384]{1,0:T(8,128)(2,1)}, u32[]{:S(2)}) copy-start(bf16[512,384]{1,0:T(8,128)(2,1)} %param.6) | copy-start | bytes 1179652
  111.2 7.0 %copy-start.4 = (s32[1,32]{1,0:T(1,128)S(1)}, s32[1,32]{1,0:T(1,128)}, u32[]{:S(2)}) copy-start(s32[1,32]{1,0:T(1,128)} %param.9) | copy-start | bytes 388
  111.2 7.8 %copy-start.5 = (s32[4]{0:T(128)S(1)}, s32[4]{0:T(128)}, u32[]{:S(2)}) copy-start(s32[4]{0:T(128)} %param.11) | copy-start | bytes 52
  111.2 355.2 %all-reduce.2.cloned.1.call-start = ((), (), s32[]{:S(2)}) async-start(), calls=%async_computation.2 | async-start | bytes 3145728 | tf_op jit(solution)/shard_map/psum | solution.py:15
  117.6 475.6 %reduce-scatter.2.cloned.1.call-start = ((), (), s32[]{:S(2)}) async-start(), calls=%async_computation.3 | async-start | bytes 3932160 | tf_op jit(solution)/shard_map/reduce_scatter | solution.py:104
  529.9 4.7 copy-start.2
Sparse Core Ops, SparseCore 0:
  117.7 348.6 all-reduce.1
  551.5 41.6 reduce-scatter.1
where the time goes:
time: 601 us; the launch traced here: 600 us
  waiting for transfers between devices  389 us (65%)
  local copies, waits for them, and re-layouts  97.3 us (16%)
  blocking collectives  46.3 us (8%)
  other arithmetic  30.8 us (5%)
  matrix products  18.6 us (3%)
  between operations  13.7 us (2%)
    psum x1, waiting for transfers between devices, from_root(): return lax.psum(jnp.where(mine, shard, jnp.zeros_like(shard)), axis)  347 us
    all_gather x1, blocking collectives, shards(): requests = lax.all_gather(fetch_list, 'tm', axis=0, tiled=True)  46.3 us
    reduce_scatter x1, waiting for transfers between devices, shards(): lax.psum_scatter(partial_value.astype(jnp.bfloat16), 'head', scatter_dime...  41.8 us
    gather x2, local copies, waits for them, and re-layouts, outgoing(): picked = jnp.take(block_rows, chosen, axis=0)  40.9 us
    gather x2, local copies, waits for them, and re-layouts, attend(): jnp.take(fetched, list_rows, axis=0).reshape(per_step, -1, 2, feature_width)  16.9 us
    slice x2, local copies, waits for them, and re-layouts, attend(): far_keys = picked[:, :, 0].reshape(per_step, -1, head_count, DH)  14.3 us
  transfers between devices with their start and end apart: 3, of which 2 were waited for; matrix products, arithmetic and copies ran while one was open for 2% of the time, Pallas kernels for 0%

commit v1 on v0

--- a/solution.py
+++ b/solution.py
@@ -43,7 +43,9 @@
     block_len = block_rows.shape[1]
     own_owners = fetch_list[0] // CB_DEV
     own_ranks = owner_ranks(own_owners)
-    requests = lax.all_gather(fetch_list, "tm", axis=0, tiled=True)
+    requests = jnp.concatenate(
+        lax.all_to_all(jnp.stack([fetch_list] * lax.axis_size("tm")), "tm", 0, 0), axis=0
+    )
     outbound = outgoing(requests, jnp.arange(CAP, dtype=jnp.int32), block_rows, me_owner)
     arrived = lax.all_to_all(outbound, "tm", split_axis=0, concat_axis=0, tiled=True)
     flat_blocks = arrived.reshape(-1, block_len, 2, feature_width)

time: 601 us -> 579 us (0.963)
  blocking collectives: 46.3 us -> 0 us
  starting transfers between devices: 4.92 us -> 18 us
  waiting for transfers between devices: 389 us -> 398 us
    all_gather x1 -> x0, blocking collectives: 46.3 us -> none  [shards(): requests = lax.all_gather(fetch_list, 'tm', axis=0, tiled=True)]
    all_to_all x0 -> x1, starting transfers between devices: none -> 12.8 us  [shards(): lax.all_to_all(jnp.stack([fetch_list] * lax.axis_size('tm')), 'tm', 0, 0)]
    all_to_all x0 -> x1, waiting for transfers between devices: none -> 9.25 us  [shards(): lax.all_to_all(jnp.stack([fetch_list] * lax.axis_size('tm')), 'tm', 0, 0)]
  transfers between devices with their start and end apart: 3 -> 4, of which waited for: 2 -> 3; matrix products, arithmetic and copies ran while one was open for 2% -> 2% of each run, Pallas kernels for 0% -> 0%
where the time goes in v1:
time: 579 us; the launch traced here: 578 us
  waiting for transfers between devices  398 us (69%)
  local copies, waits for them, and re-layouts  98.7 us (17%)
  other arithmetic  30.9 us (5%)
  matrix products  18.6 us (3%)
  starting transfers between devices  18 us (3%)
  between operations  13.7 us (2%)
    psum x1, waiting for transfers between devices, from_root(): return lax.psum(jnp.where(mine, shard, jnp.zeros_like(shard)), axis)  348 us
    gather x2, local copies, waits for them, and re-layouts, outgoing(): picked = jnp.take(block_rows, chosen, axis=0)  40.9 us
    reduce_scatter x1, waiting for transfers between devices, shards(): lax.psum_scatter(partial_value.astype(jnp.bfloat16), 'head', scatter_dime...  40.6 us
    gather x2, local copies, waits for them, and re-layouts, attend(): jnp.take(fetched, list_rows, axis=0).reshape(per_step, -1, 2, feature_width)  16.9 us
    slice x2, local copies, waits for them, and re-layouts, attend(): far_keys = picked[:, :, 0].reshape(per_step, -1, head_count, DH)  14.3 us
    all_to_all x1, starting transfers between devices, shards(): lax.all_to_all(jnp.stack([fetch_list] * lax.axis_size('tm')), 'tm', 0, 0)  12.8 us
  transfers between devices with their start and end apart: 4, of which 3 were waited for; matrix products, arithmetic and copies ran while one was open for 2% of the time, Pallas kernels for 0%

profile of v1, /device:TPU:1, one launch (start us, length us, event | category | flops | bytes accessed | tf_op | source)
XLA Modules:
  0.0 577.9 jit_solution(4613395941587107165)
XLA Ops:
  8.0 12.8 %all-to-all-start = ((s32[32,1,32]{2,1,0:T(1,128)}), s32[32,1,32]{2,1,0:T(1,128)S(1)}, u32[]{:S(2)}, u32[]{:S(2)}) async-start(s32[32,1,32]{2,1,0:T(1,128)} %stack.2), calls=%async_computation | async-start | bytes 32768 | tf_op jit(solution)/shard_map/all_to_all | solution.py:47
  20.7 9.3 %all-to-all-done = s32[32,1,32]{2,1,0:T(1,128)S(1)} async-done(((s32[32,1,32]{2,1,0:T(1,128)}), s32[32,1,32]{2,1,0:T(1,128)S(1)}, u32[]{:S(2)}, u32[]{:S(2)}) %all-to-all-start) | async-done | bytes 4128 | tf_op jit(solution)/shard_map/all_to_all | solution.py:47
  31.4 29.4 %gather_fusion = bf16[64,128,2,384]{3,2,1,0:T(2,128)(2,1)} fusion(bf16[8,128,2,384]{3,2,1,0:T(2,128)(2,1)} %bitcast.95, s32[1024]{0:T(1024)S(1)} %pad_clamp_fusion.2), kind=kCustom, calls=%fused_computation | custom fusion | bytes 25166080 | tf_op jit(solution)/shard_map/jit(_take)/gather | solution.py:34
  60.8 11.5 %copy.138 = bf16[64,128,2,384]{3,1,2,0:T(8,128)(2,1)} copy(bf16[64,128,2,384]{3,2,1,0:T(2,128)(2,1)} %gather_fusion) | data formatting | bytes 25165824 | tf_op jit(solution)/shard_map/jit(_take)/gather | solution.py:34
  72.5 11.0 %select_select_fusion = bf16[32,2,128,2,384]{4,2,3,1,0:T(8,128)(2,1)} fusion(bf16[32,2,128,2,384]{4,2,3,1,0:T(8,128)(2,1)} %bitcast.96, pred[32,2]{1,0:T(8,128)(4,1)S(1)} %copy.136, pred[32,2]{1,0:T(8,128)(4,1)S(1)} %copy.135), kind=kLoop, calls=%fused_computation.7 | loop fusion | flops 12582912 | bytes 25165952 | tf_op jit(solution)/shard_map/jit(_where)/select_n | solution.py:35
  83.6 5.2 all-to-all-start.1
  88.9 5.0 copy.145
  97.3 348.2 %all-reduce.2.cloned.1.call-done = bf16[1024,2,384]{0,2,1:T(8,128)(2,1)} async-done(((bf16[1024,2,384]{0,2,1:T(8,128)(2,1)}), bf16[1024,2,384]{0,2,1:T(8,128)(2,1)}) %all-reduce.2.cloned.1.call-update) | async-done | bytes 1572880 | tf_op jit(solution)/shard_map/psum | solution.py:15
  445.4 1.5 fusion.42
  446.9 4.3 fusion.9
  451.2 8.7 %gather_fusion.1 = bf16[32,128,2,384]{3,1,2,0:T(8,128)(2,1)} fusion(bf16[64,128,2,384]{3,1,2,0:T(8,128)(2,1)} %bitcast.7, s32[1024]{0:T(1024)} %pad_clamp_fusion.1), kind=kCustom, calls=%fused_computation.1 | custom fusion | bytes 12583040 | tf_op jit(solution)/shard_map/jit(_take)/gather | solution.py:52
  460.0 6.2 %broadcast_select_fusion = bf16[32,128,2,384]{3,1,2,0:T(8,128)(2,1)} fusion(bf16[32,128,2,384]{3,1,2,0:T(8,128)(2,1)} %gather_fusion.1, pred[32]{0:T(512)(128)(4,1)} %compare_and_fusion.1), kind=kLoop, calls=%fused_computation.15 | loop fusion | flops 3145728 | bytes 12582944 | tf_op jit(solution)/shard_map/jit(_take)/select_n | solution.py:52
  466.1 9.9 %gather_fusion.2 = bf16[64,128,2,384]{3,1,2,0:T(8,128)(2,1)} fusion(bf16[32,128,2,384]{3,1,2,0:T(8,128)(2,1)} %broadcast_select_fusion, s32[1024]{0:T(1024)S(1)} %pad_clamp_fusion), kind=kCustom, calls=%fused_computation.2 | custom fusion | bytes 25166080 | tf_op jit(solution)/shard_map/while/body/eval_jaxpr/jit(_take)/gather | solution.py:68
  476.0 7.0 %copy.139 = bf16[64,128,2,384]{3,1,0,2:T(8,128)(2,1)S(1)} copy(bf16[64,128,2,384]{3,1,2,0:T(8,128)(2,1)} %gather_fusion.2) | data formatting | bytes 25165824 | tf_op jit(solution)/shard_map/while/body/eval_jaxpr/jit(_take)/gather | solution.py:68
  483.0 3.0 bitcast_select_fusion
  486.0 5.7 fusion.41
  491.7 8.7 %copy.140 = bf16[4,2048,1,384]{1,3,0,2:T(8,128)(2,1)} copy(bf16[4,2048,1,384]{3,1,0,2:T(8,128)(2,1)} %get-tuple-element.24) | data formatting | bytes 12582912 | tf_op jit(solution)/shard_map/while/body/eval_jaxpr/slice | solution.py:70
  500.4 8.6 %copy.141 = bf16[4,2048,1,384]{1,3,0,2:T(8,128)(2,1)} copy(bf16[4,2048,1,384]{3,1,0,2:T(8,128)(2,1)} %get-tuple-element.23) | data formatting | bytes 12582912 | tf_op jit(solution)/shard_map/while/body/eval_jaxpr/slice | solution.py:69
  509.0 4.7 bitcast_reduce_fusion
  513.7 2.1 fusion.1
  515.8 5.4 fusion.12
  521.2 4.7 fusion.7
  526.9 3.5 convolution_convert_fusion
  530.5 40.6 %reduce-scatter.2.cloned.1.call-done = bf16[512,768]{1,0:T(8,128)(2,1)} async-done(((bf16[512,3072]{1,0:T(8,128)(2,1)}), bf16[512,768]{1,0:T(8,128)(2,1)}) %reduce-scatter.2.cloned.1.call-update) | async-done | bytes 786448 | tf_op jit(solution)/shard_map/reduce_scatter | solution.py:106
  (54 shorter events, 7.3 us)
Async XLA Ops:
  6.5 520.4 %copy-start = (bf16[384,3072]{1,0:T(8,128)(2,1)S(1)}, bf16[384,3072]{1,0:T(8,128)(2,1)}, u32[]{:S(2)}) copy-start(bf16[384,3072]{1,0:T(8,128)(2,1)} %param.8) | copy-start | bytes 7077892
  8.0 22.0 %all-to-all-start = ((s32[32,1,32]{2,1,0:T(1,128)}), s32[32,1,32]{2,1,0:T(1,128)S(1)}, u32[]{:S(2)}, u32[]{:S(2)}) async-start(s32[32,1,32]{2,1,0:T(1,128)} %stack.2), calls=%async_computation | async-start | bytes 32768 | tf_op jit(solution)/shard_map/all_to_all | solution.py:47
  83.6 367.7 %all-to-all-start.1 = ((bf16[32,2,128,2,384]{4,2,3,1,0:T(8,128)(2,1)}), bf16[32,2,128,2,384]{4,2,3,1,0:T(8,128)(2,1)}, u32[]{:S(2)}, u32[]{:S(2)}) async-start(bf16[32,2,128,2,384]{4,2,3,1,0:T(8,128)(2,1)} %select_select_fusion), calls=%async_computation.1 | async-start | bytes 25165824 | tf_op jit(solution)/shard_map/all_to_all | solution.py:50
  88.8 6.5 %copy-start.3 = (s32[4,16]{1,0:T(4,128)S(1)}, s32[4,16]{1,0:T(4,128)}, u32[]{:S(2)}) copy-start(s32[4,16]{1,0:T(4,128)} %param.10) | copy-start | bytes 772
  88.8 6.7 %copy-start.1 = (bf16[512,384]{1,0:T(8,128)(2,1)S(1)}, bf16[512,384]{1,0:T(8,128)(2,1)}, u32[]{:S(2)}) copy-start(bf16[512,384]{1,0:T(8,128)(2,1)} %param.6) | copy-start | bytes 1179652
  88.8 7.0 %copy-start.4 = (s32[1,32]{1,0:T(1,128)S(1)}, s32[1,32]{1,0:T(1,128)}, u32[]{:S(2)}) copy-start(s32[1,32]{1,0:T(1,128)} %param.9) | copy-start | bytes 388
  88.8 7.8 %copy-start.5 = (s32[4]{0:T(128)S(1)}, s32[4]{0:T(128)}, u32[]{:S(2)}) copy-start(s32[4]{0:T(128)} %param.11) | copy-start | bytes 52
  88.8 356.6 %all-reduce.2.cloned.1.call-start = ((), (), s32[]{:S(2)}) async-start(), calls=%async_computation.3 | async-start | bytes 3145728 | tf_op jit(solution)/shard_map/psum | solution.py:15
  95.2 475.8 %reduce-scatter.2.cloned.1.call-start = ((), (), s32[]{:S(2)}) async-start(), calls=%async_computation.4 | async-start | bytes 3932160 | tf_op jit(solution)/shard_map/reduce_scatter | solution.py:106
  509.0 4.7 copy-start.2
Sparse Core Ops, SparseCore 0:
  95.3 350.0 all-reduce.1
  530.6 40.3 reduce-scatter.1
